TPU v7x, 256 devices: a whole 4x4x8 slice. The times are simulated.
256 devices in a mesh: blk: 16 (over z, x_hi), leaf: 8 (over y, core), rhs: 2 (over x_lo).
Axes of the slice: x: 4 (x_hi: 2, x_lo: 2; x = x_hi * 2 + x_lo), y: 4, z: 8, core: 2. Of those that a mesh axis runs over, the one named last changes fastest.
Arguments:
- residual: float32 [32, 8, 65536], P('rhs', 'leaf', 'blk'), may hold values from -160 to 160
- points: float32 [3, 8, 65536], P(None, 'leaf', 'blk'), may hold values from -12330 to 12330
- noise: float32 [8, 65536], P('leaf', 'blk'), may hold values from 1 to 2
- block_list: int32 [8, 8, 256], P('leaf'), may hold values from 0 to 1, as said below
Outputs:
- correction: float32 [32, 8, 65536], P('rhs', 'leaf', 'blk')
- new_residual: float32 [32, 8, 65536], P('rhs', 'leaf', 'blk')
- basis: float32 [128, 8, 65536], P('rhs', 'leaf', 'blk')
Inputs may be any that keep to these rules, and one draw needn't show every extreme that they name: The list is symmetric: block_list[t, k, i] == block_list[t, 7 - k, (i + d) mod 256] with d the offset of entry k.
All inputs are finite; a program needn't handle non-finite values.
Results may differ from a plain program's by a relative error of at most 0.007.
Values sent between devices are 32-bit elements; how exact they have to be, the bound alone decides.
A program may use at most 128 MiB of HBM per device.

v0:
```python
import jax
import jax.numpy as jnp
from jax import lax
from jax.sharding import PartitionSpec as P

M = 32
S = 4
BS = 256
REACH = 4
SUPPORT = 1408
centre_shift = 1.5
amplitude = 1.1
exact = lax.Precision.HIGHEST


def extended(x, sides, width):
    for axis, dim in sides:
        count, length = (lax.axis_size(axis), x.shape[dim])
        up = [(i, (i + 1) % count) for i in range(count)]
        down = [(j, i) for i, j in up]
        last = lax.slice_in_dim(x, length - width, length, axis=dim)
        leading = lax.slice_in_dim(x, 0, width, axis=dim)
        before = lax.ppermute(last, axis, up)
        after = lax.ppermute(leading, axis, down)
        x = jnp.concatenate([before, x, after], axis=dim)
    return x


def kernel_tile(near_points, own_points):
    squared = (near_points[0][:, None] - own_points[0][None, :]) ** 2
    squared = squared + (near_points[1][:, None] - own_points[1][None, :]) ** 2
    squared = squared + (near_points[2][:, None] - own_points[2][None, :]) ** 2
    radius = jnp.sqrt(squared) / SUPPORT
    remain = jnp.maximum(1.0 - radius, 0.0)
    return remain * remain * (remain * remain) * (4.0 * radius + 1.0) * (amplitude / SUPPORT)


def band_product(field_wide, points_wide, weights, rows_out):
    per_turn = rows_out // 8
    count = field_wide.shape[0]

    def turn(carry, index):
        pieces = []
        for inner in range(per_turn):
            block = index * per_turn + inner
            own_points = lax.dynamic_slice_in_dim(points_wide, (block + REACH) * BS, BS, 1)
            total = jnp.zeros((count, BS), jnp.float32)
            for offset in range(2 * REACH + 1):
                column_at = (block + offset) * BS
                near_points = lax.dynamic_slice_in_dim(points_wide, column_at, BS, 1)
                near_field = lax.dynamic_slice_in_dim(field_wide, column_at, BS, 1)
                listed = lax.dynamic_index_in_dim(weights[offset], block, 0, False)
                tile = kernel_tile(near_points, own_points) * listed
                total = total + jnp.dot(near_field, tile, precision=exact)
            pieces.append(total)
        return (carry, jnp.concatenate(pieces, axis=1))

    carry, parts = lax.scan(turn, jnp.zeros((), jnp.int32), jnp.arange(8, dtype=jnp.int32))
    return jnp.moveaxis(parts, 0, 1).reshape(count, rows_out * BS)


def galerkin(gram, count_points, count_sides):
    normed = gram / count_points
    basis_count = normed.shape[0] - count_sides
    gram_basis = normed[:basis_count, :basis_count]
    factor_low = jnp.linalg.cholesky(gram_basis)
    inverse_low = lax.linalg.triangular_solve(
        factor_low, jnp.eye(basis_count, dtype=jnp.float32), left_side=True, lower=True
    )
    cross = normed[:basis_count, count_sides:] + centre_shift * gram_basis
    projected = jnp.dot(
        jnp.dot(inverse_low, cross, precision=exact), inverse_low.T, precision=exact
    )
    projected = 0.5 * (projected + projected.T)
    small_side = jnp.dot(inverse_low, gram_basis[:, :count_sides], precision=exact)
    proj_factor = jnp.linalg.cholesky(projected)
    halfway = lax.linalg.triangular_solve(proj_factor, small_side, left_side=True, lower=True)
    coeffs = lax.linalg.triangular_solve(
        proj_factor, halfway, left_side=True, lower=True, transpose_a=True
    )
    combo = jnp.dot(coeffs.T, inverse_low, precision=exact)
    return (inverse_low, combo)


def row_products(rows):
    return lax.dot_general(rows, rows, (((1,), (1,)), ((), ())), precision=exact)


def local(residual, points, noise, block_list):
    field = residual[:, 0]
    coords = points[:, 0]
    nugget = noise[0]
    own_rows = field.shape[1]
    own_blocks = own_rows // BS
    first_block = lax.axis_index("blk") * own_blocks
    listed = block_list[0].astype(jnp.float32)
    nine = jnp.concatenate(
        [listed[:REACH], jnp.ones((1, listed.shape[1]), jnp.float32), listed[REACH:]], axis=0
    )
    margin = S * REACH
    wrapped = jnp.concatenate([nine[:, -margin:], nine, nine[:, :margin]], axis=1)
    powers = [field]
    rim = REACH * BS
    coords_wide = extended(coords, (("blk", 1),), rim)
    own_weights = lax.dynamic_slice_in_dim(wrapped, first_block + margin, own_blocks, 1)
    current = field
    for power_step in range(S):
        widened = extended(current, (("blk", 1),), rim)
        current = (
            band_product(widened, coords_wide, own_weights, own_blocks)
            + (nugget - centre_shift) * current
        )
        powers.append(current)
    half_panel = jnp.stack(powers, axis=0)
    count_points = own_rows * lax.axis_size("blk") * lax.axis_size("leaf")
    sides_here = field.shape[0]
    whole = lax.all_gather(half_panel, "rhs", axis=1, tiled=True)
    flat = whole.reshape(-1, own_rows)
    gram = lax.psum(row_products(flat), ("blk", "leaf"))
    inverse_low, combo = galerkin(gram, count_points, M)
    first_rows = flat[: S * M]
    image = flat[M:] + centre_shift * first_rows
    part = lax.axis_index("rhs")
    basis_here = S * M // lax.axis_size("rhs")
    mine_low = lax.dynamic_slice_in_dim(inverse_low, part * basis_here, basis_here, 0)
    mine_combo = lax.dynamic_slice_in_dim(combo, part * sides_here, sides_here, 0)
    correction = jnp.dot(mine_combo, first_rows, precision=exact)
    new_residual = field - jnp.dot(mine_combo, image, precision=exact)
    basis = jnp.dot(mine_low, first_rows, precision=exact)
    return (correction[:, None], new_residual[:, None], basis[:, None])


def solution(mesh):
    placed = (
        P("rhs", "leaf", "blk"),
        P(None, "leaf", "blk"),
        P("leaf", "blk"),
        P("leaf", None, None),
    )
    return jax.shard_map(
        local,
        mesh=mesh,
        in_specs=placed,
        out_specs=(P("rhs", "leaf", "blk"), P("rhs", "leaf", "blk"), P("rhs", "leaf", "blk")),
        check_vma=False,
    )
```

profile of v0, /device:TPU:2, one launch (start us, length us, event | category | flops | bytes accessed | tf_op | source)
XLA Modules:
  0.0 2114.2 jit_solution(17787421845742051918)
XLA Ops:
  7.2 0.8 copy.48
  8.1 2.2 collective-permute-start.2
  10.3 5.4 collective-permute-start.3
  15.6 1.1 copy.47
  16.9 5.6 collective-permute-start.1
  22.5 1.1 bitcast_dynamic-update-slice_fusion
  23.6 0.7 convert_element_type.5
  24.4 0.7 broadcast_add_fusion
  25.4 206.0 %while.52 = (s32[]{:T(128)}, f32[8,16,512]{2,1,0:T(8,128)S(1)}, s32[8]{0:T(128)S(1)}, f32[16,6144]{1,0:T(8,128)S(1)}, f32[3,6144]{1,0:T(4,128)S(1)}, /*index=5*/...) while((s32[]{:T(128)}, f32[8,16,512]{2,1,0:T(8,128)S(1)}, ...), condition=%wide.region_1.2_spmd, body=%wide.region_0.1_spmd.sunk | while | flops 246620224 | bytes 1092197 | solution.py:58
  38.6 0.7 constant_dynamic-slice_fusion.141
  64.3 0.7 constant_dynamic-slice_fusion.141
  167.3 0.7 constant_dynamic-slice_fusion.141
  193.0 0.7 constant_dynamic-slice_fusion.141
  231.9 5.6 collective-permute-start.5
  237.9 1.8 collective-permute-done.4
  239.8 202.8 %while.53 = (s32[]{:T(128)}, f32[8,16,512]{2,1,0:T(8,128)S(1)}, s32[8]{0:T(128)S(1)}, f32[16,6144]{1,0:T(8,128)S(1)}, f32[3,6144]{1,0:T(4,128)S(1)}, /*index=5*/...) while((s32[]{:T(128)}, f32[8,16,512]{2,1,0:T(8,128)S(1)}, ...), condition=%wide.region_3.4_spmd, body=%wide.region_2.3_spmd.sunk | while | flops 246620224 | bytes 1092197 | solution.py:58
  442.8 6.1 collective-permute-start.7
  449.2 1.5 collective-permute-done.6
  450.9 203.8 %while.54 = (s32[]{:T(128)}, f32[8,16,512]{2,1,0:T(8,128)S(1)}, s32[8]{0:T(128)S(1)}, f32[16,6144]{1,0:T(8,128)S(1)}, f32[3,6144]{1,0:T(4,128)S(1)}, /*index=5*/...) while((s32[]{:T(128)}, f32[8,16,512]{2,1,0:T(8,128)S(1)}, ...), condition=%wide.region_5.6_spmd, body=%wide.region_4.5_spmd.sunk | while | flops 246620224 | bytes 1092197 | solution.py:58
  654.8 1.9 collective-permute-start.8
  656.7 4.4 collective-permute-start.9
  661.4 1.8 collective-permute-done.8
  663.4 207.7 %while.55 = (s32[]{:T(128)}, f32[8,16,512]{2,1,0:T(8,128)S(1)}, s32[8]{0:T(128)S(1)}, f32[16,6144]{1,0:T(8,128)S(1)}, f32[3,6144]{1,0:T(4,128)S(1)}, /*index=5*/...) while((s32[]{:T(128)}, f32[8,16,512]{2,1,0:T(8,128)S(1)}, ...), condition=%wide.region_7.8_spmd, body=%wide.region_6.7_spmd.sunk | while | flops 246620224 | bytes 1092197 | solution.py:58
  676.8 0.7 constant_dynamic-slice_fusion.159
  702.7 0.7 constant_dynamic-slice_fusion.159
  728.7 0.7 constant_dynamic-slice_fusion.159
  754.7 0.7 constant_dynamic-slice_fusion.159
  780.6 0.7 constant_dynamic-slice_fusion.159
  806.6 0.7 constant_dynamic-slice_fusion.159
  832.5 0.7 constant_dynamic-slice_fusion.159
  858.5 0.7 constant_dynamic-slice_fusion.159
  871.3 1.0 copy-done.4
  872.7 45.1 %all-gather.2.cloned.1.call-done = f32[5,32,4096]{2,1,0:T(8,128)} async-done(((f32[5,16,4096]{2,1,0:T(8,128)}), f32[5,32,4096]{2,1,0:T(8,128)}) %all-gather.2.cloned.1.call-update) | async-done | bytes 2621456 | tf_op jit(solution)/shard_map/all_gather | solution.py:117
  917.8 5.6 fusion.2577
  923.9 1.3 copy-done.1
  925.2 1.6 bitcast_add_fusion
  926.8 1122.0 %all-reduce.2.cloned.1.call-done = f32[160,160]{0,1:T(8,128)} async-done(((f32[160,160]{0,1:T(8,128)}), f32[160,160]{0,1:T(8,128)}) %all-reduce.2.cloned.1.call-update) | async-done | bytes 102416 | tf_op jit(solution)/shard_map/psum | solution.py:119
  2048.8 0.9 broadcast_multiply_fusion
  2049.9 11.7 cholesky.44
  2062.9 9.8 custom-call.10
  2074.0 12.0 cholesky.55
  2087.3 9.8 custom-call.11
  2097.8 2.7 fusion.2532
  2100.6 1.0 copy.29
  2101.6 1.1 convolution_bitcast_fusion.1
  2102.7 1.2 convolution_bitcast_fusion
  2103.9 2.0 copy.30
  2105.9 1.0 copy.28
  (936 shorter events, 413.4 us)
Async XLA Ops:
  7.2 910.6 %all-gather.2.cloned.1.call-start = ((), (), s32[]{:S(2)}) async-start(), calls=%async_computation | async-start | bytes 3932160 | tf_op jit(solution)/shard_map/all_gather | solution.py:117
  8.1 17.2 collective-permute-start.2
  10.3 15.0 collective-permute-start.3
  16.8 8.5 collective-permute-start
  16.9 8.4 collective-permute-start.1
  25.4 206.0 %copy-start.3 = (f32[16,1,4096]{2,1,0:T(1,128)S(1)}, f32[16,1,4096]{2,1,0:T(1,128)}, u32[]{:S(2)}) copy-start(f32[16,1,4096]{2,1,0:T(1,128)} %param.13) | copy-start | bytes 786436
  231.6 8.2 collective-permute-start.4
  231.9 7.9 collective-permute-start.5
  442.7 8.0 collective-permute-start.6
  442.8 8.0 collective-permute-start.7
  654.8 8.4 collective-permute-start.8
  656.7 6.6 collective-permute-start.9
  871.3 1.1 copy-start.4
  872.4 1176.4 %all-reduce.2.cloned.1.call-start = ((), (), s32[]{:S(2)}) async-start(), calls=%async_computation.1 | async-start | bytes 327680 | tf_op jit(solution)/shard_map/psum | solution.py:119
  917.8 5.6 copy-start
  923.9 1.3 copy-start.1
  2073.9 27.7 %copy-start.2 = (f32[4,32,4096]{2,1,0:T(8,128)S(1)}, f32[4,32,4096]{2,1,0:T(8,128)}, u32[]{:S(2)}) copy-start(f32[4,32,4096]{2,1,0:T(8,128)} %copy-done.1) | copy-start | bytes 6291460
Sparse Core Ops, SparseCore 0:
  872.5 45.1 all-gather.1
  923.5 1125.2 all-reduce.1
where the time goes:
time: 2130 us; the launch traced here: 2110 us
  waiting for transfers between devices  1170 us (55%)
  loops' own time  407 us (19%)
  matrix products  296 us (14%)
  local copies, waits for them, and re-layouts  140 us (7%)
  other arithmetic  51.7 us (2%)
  starting transfers between devices  32 us (2%)
    psum x1, waiting for transfers between devices, local(): gram = lax.psum(row_products(flat), ('blk', 'leaf'))  1120 us
    another operation x4, loops' own time, band_product(): lax.scan(turn, jnp.zeros((), jnp.int32), jnp.arange(8, dtype=jnp.int32))  407 us
    dot_general x576, matrix products, turn(): total = total + jnp.dot(near_field, tile, precision=exact)  284 us
    dynamic_slice x160, local copies, waits for them, and re-layouts, turn(): listed = lax.dynamic_index_in_dim(weights[offset], block, 0, False)  105 us
    all_gather x1, waiting for transfers between devices, local(): whole = lax.all_gather(half_panel, 'rhs', axis=1, tiled=True)  45.1 us
  transfers between devices with their start and end apart: 12, of which 7 were waited for; matrix products, arithmetic and copies ran while one was open for 0% of the time, Pallas kernels for 0%

commit v1 on v0

--- a/solution.py
+++ b/solution.py
@@ -116,7 +116,8 @@
     sides_here = field.shape[0]
     whole = lax.all_gather(half_panel, "rhs", axis=1, tiled=True)
     flat = whole.reshape(-1, own_rows)
-    gram = lax.psum(row_products(flat), ("blk", "leaf"))
+    one_axis = lax.psum(row_products(flat), "leaf")
+    gram = lax.psum(one_axis, "blk")
     inverse_low, combo = galerkin(gram, count_points, M)
     first_rows = flat[: S * M]
     image = flat[M:] + centre_shift * first_rows

time: 2130 us -> 1230 us (0.58)
  waiting for transfers between devices: 1170 us -> 267 us
    psum x1 -> x2, waiting for transfers between devices: 1120 us -> 217 us  [the longest x1 154 us: local(): gram = lax.psum(one_axis, 'blk')]
  transfers between devices with their start and end apart: 12 -> 13, of which waited for: 7 -> 8; matrix products, arithmetic and copies ran while one was open for 0% -> 1% of each run, Pallas kernels for 0% -> 0%
where the time goes in v1:
time: 1230 us; the launch traced here: 1220 us
  loops' own time  411 us (33%)
  matrix products  296 us (24%)
  waiting for transfers between devices  267 us (22%)
  local copies, waits for them, and re-layouts  142 us (12%)
  other arithmetic  53.9 us (4%)
  starting transfers between devices  32.1 us (3%)
  between operations  14.7 us (1%)
    another operation x4, loops' own time, band_product(): lax.scan(turn, jnp.zeros((), jnp.int32), jnp.arange(8, dtype=jnp.int32))  411 us
    dot_general x576, matrix products, turn(): total = total + jnp.dot(near_field, tile, precision=exact)  284 us
    psum x1, waiting for transfers between devices, local(): gram = lax.psum(one_axis, 'blk')  154 us
    dynamic_slice x160, local copies, waits for them, and re-layouts, turn(): listed = lax.dynamic_index_in_dim(weights[offset], block, 0, False)  105 us
    psum x1, waiting for transfers between devices, local(): one_axis = lax.psum(row_products(flat), 'leaf')  62.5 us
    all_gather x1, waiting for transfers between devices, local(): whole = lax.all_gather(half_panel, 'rhs', axis=1, tiled=True)  45.3 us
    ppermute x5, starting transfers between devices, extended(): after = lax.ppermute(leading, axis, down)  27.2 us
  transfers between devices with their start and end apart: 13, of which 8 were waited for; matrix products, arithmetic and copies ran while one was open for 1% of the time, Pallas kernels for 0%

profile of v1, /device:TPU:2, one launch (start us, length us, event | category | flops | bytes accessed | tf_op | source)
XLA Modules:
  0.0 1217.0 jit_solution(10102002933254784757)
XLA Ops:
  7.2 0.8 copy.48
  8.1 2.2 collective-permute-start.2
  10.3 5.4 collective-permute-start.3
  15.6 1.1 copy.47
  16.9 5.6 collective-permute-start.1
  22.5 1.1 bitcast_dynamic-update-slice_fusion
  23.6 0.7 convert_element_type.5
  24.4 0.7 broadcast_add_fusion
  25.4 204.8 %while.52 = (s32[]{:T(128)}, f32[8,16,512]{2,1,0:T(8,128)S(1)}, s32[8]{0:T(128)S(1)}, f32[16,6144]{1,0:T(8,128)S(1)}, f32[3,6144]{1,0:T(4,128)S(1)}, /*index=5*/...) while((s32[]{:T(128)}, f32[8,16,512]{2,1,0:T(8,128)S(1)}, ...), condition=%wide.region_1.2_spmd, body=%wide.region_0.1_spmd.sunk | while | flops 246620224 | bytes 1092197 | solution.py:58
  230.8 5.6 collective-permute-start.5
  236.8 1.8 collective-permute-done.4
  238.7 205.5 %while.53 = (s32[]{:T(128)}, f32[8,16,512]{2,1,0:T(8,128)S(1)}, s32[8]{0:T(128)S(1)}, f32[16,6144]{1,0:T(8,128)S(1)}, f32[3,6144]{1,0:T(4,128)S(1)}, /*index=5*/...) while((s32[]{:T(128)}, f32[8,16,512]{2,1,0:T(8,128)S(1)}, ...), condition=%wide.region_3.4_spmd, body=%wide.region_2.3_spmd.sunk | while | flops 246620224 | bytes 1092197 | solution.py:58
  277.8 0.7 constant_dynamic-slice_fusion.147
  329.2 0.7 constant_dynamic-slice_fusion.147
  406.2 0.7 constant_dynamic-slice_fusion.147
  444.4 6.1 collective-permute-start.7
  450.8 1.5 collective-permute-done.6
  452.5 208.4 %while.54 = (s32[]{:T(128)}, f32[8,16,512]{2,1,0:T(8,128)S(1)}, s32[8]{0:T(128)S(1)}, f32[16,6144]{1,0:T(8,128)S(1)}, f32[3,6144]{1,0:T(4,128)S(1)}, /*index=5*/...) while((s32[]{:T(128)}, f32[8,16,512]{2,1,0:T(8,128)S(1)}, ...), condition=%wide.region_5.6_spmd, body=%wide.region_4.5_spmd.sunk | while | flops 246620224 | bytes 1092197 | solution.py:58
  466.0 0.7 constant_dynamic-slice_fusion.153
  492.1 0.7 constant_dynamic-slice_fusion.153
  518.1 0.7 constant_dynamic-slice_fusion.153
  544.2 0.7 constant_dynamic-slice_fusion.153
  570.2 0.7 constant_dynamic-slice_fusion.153
  596.3 0.7 constant_dynamic-slice_fusion.153
  622.3 0.7 constant_dynamic-slice_fusion.153
  648.4 0.7 constant_dynamic-slice_fusion.153
  661.0 1.9 collective-permute-start.8
  662.9 4.4 collective-permute-start.9
  667.6 1.8 collective-permute-done.8
  669.6 206.8 %while.55 = (s32[]{:T(128)}, f32[8,16,512]{2,1,0:T(8,128)S(1)}, s32[8]{0:T(128)S(1)}, f32[16,6144]{1,0:T(8,128)S(1)}, f32[3,6144]{1,0:T(4,128)S(1)}, /*index=5*/...) while((s32[]{:T(128)}, f32[8,16,512]{2,1,0:T(8,128)S(1)}, ...), condition=%wide.region_7.8_spmd, body=%wide.region_6.7_spmd.sunk | while | flops 246620224 | bytes 1092197 | solution.py:58
  876.7 1.1 copy-done.3
  877.8 45.3 %all-gather.2.cloned.1.call-done = f32[5,32,4096]{2,1,0:T(8,128)} async-done(((f32[5,16,4096]{2,1,0:T(8,128)}), f32[5,32,4096]{2,1,0:T(8,128)}) %all-gather.2.cloned.1.call-update) | async-done | bytes 2621456 | tf_op jit(solution)/shard_map/all_gather | solution.py:117
  923.1 5.6 fusion.2577
  929.0 2.6 fusion.2570
  931.6 62.5 %all-reduce.3.cloned.1.call-done = f32[160,160]{0,1:T(8,128)} async-done(((f32[160,160]{0,1:T(8,128)}), f32[160,160]{0,1:T(8,128)}) %all-reduce.3.cloned.1.call-update) | async-done | bytes 102416 | tf_op jit(solution)/shard_map/psum | solution.py:119
  994.1 3.9 bitcast_add_fusion
  998.0 154.0 %all-reduce.5.cloned.1.call-done = f32[160,160]{0,1:T(8,128)} async-done(((f32[160,160]{0,1:T(8,128)}), f32[160,160]{0,1:T(8,128)}) %all-reduce.5.cloned.1.call-update) | async-done | bytes 102416 | tf_op jit(solution)/shard_map/psum | solution.py:120
  1152.0 0.9 broadcast_multiply_fusion
  1153.1 11.7 cholesky.44
  1166.1 9.8 custom-call.10
  1177.2 11.7 cholesky.55
  1190.2 10.0 custom-call.11
  1201.0 2.7 fusion.2532
  1203.7 1.0 copy.29
  1204.7 1.1 convolution_bitcast_fusion.1
  1205.8 1.2 convolution_bitcast_fusion
  1207.0 2.0 copy.30
  1209.1 1.0 copy.28
  (937 shorter events, 414.9 us)
Async XLA Ops:
  7.2 916.0 %all-gather.2.cloned.1.call-start = ((), (), s32[]{:S(2)}) async-start(), calls=%async_computation | async-start | bytes 3932160 | tf_op jit(solution)/shard_map/all_gather | solution.py:117
  8.1 17.2 %collective-permute-start.2 = (f32[3,1024]{1,0:T(4,128)S(1)}, f32[3,1024]{1,0:T(4,128)S(1)}, u32[]{:S(2)}, u32[]{:S(2)}) collective-permute-start(f32[3,1024]{1,0:T(4,128)S(1)} %get-tuple-element.898), channel_id=1, source_target_pairs={{0,16},{16,32},{32,48},{48,64},{64,80},{80,96},{96,112},{112,128},... | collective-permute-start | bytes 36872 | tf_op jit(solution)/shard_map/ppermute | solution.py:23
  10.3 15.0 %collective-permute-start.3 = (f32[3,1024]{1,0:T(4,128)S(1)}, f32[3,1024]{1,0:T(4,128)S(1)}, u32[]{:S(2)}, u32[]{:S(2)}) collective-permute-start(f32[3,1024]{1,0:T(4,128)S(1)} %get-tuple-element.899), channel_id=1, source_target_pairs={{16,0},{32,16},{48,32},{64,48},{80,64},{96,80},{112,96},{128,112},... | collective-permute-start | bytes 36872 | tf_op jit(solution)/shard_map/ppermute | solution.py:24
  16.8 8.5 collective-permute-start
  16.9 8.4 collective-permute-start.1
  25.4 204.9 %copy-start.2 = (f32[16,1,4096]{2,1,0:T(1,128)S(1)}, f32[16,1,4096]{2,1,0:T(1,128)}, u32[]{:S(2)}) copy-start(f32[16,1,4096]{2,1,0:T(1,128)} %param.13) | copy-start | bytes 786436
  230.5 8.2 collective-permute-start.4
  230.8 7.9 collective-permute-start.5
  444.3 8.0 collective-permute-start.6
  444.4 8.0 collective-permute-start.7
  661.0 8.4 collective-permute-start.8
  662.9 6.6 collective-permute-start.9
  876.7 1.1 copy-start.3
  877.8 116.3 %all-reduce.3.cloned.1.call-start = ((), (), s32[]{:S(2)}) async-start(), calls=%async_computation.1 | async-start | bytes 327680 | tf_op jit(solution)/shard_map/psum | solution.py:119
  923.1 5.9 copy-start
  928.8 223.2 %all-reduce.5.cloned.1.call-start = ((), (), s32[]{:S(2)}) async-start(), calls=%async_computation.2 | async-start | bytes 327680 | tf_op jit(solution)/shard_map/psum | solution.py:120
  1177.1 27.7 %copy-start.1 = (f32[4,32,4096]{2,1,0:T(8,128)S(1)}, f32[4,32,4096]{2,1,0:T(8,128)}, u32[]{:S(2)}) copy-start(f32[4,32,4096]{2,1,0:T(8,128)} %get-tuple-element.889) | copy-start | bytes 6291460
Sparse Core Ops, SparseCore 0:
  877.9 45.1 all-gather.1
  928.9 65.1 all-reduce.2
  996.9 155.0 all-reduce.4
